TPU v7x, 32 devices: a whole 2x2x4 slice. The times are simulated.
32 devices in a mesh: req: 4 (over z), head: 2 (over core), exp: 4 (over y, x).
Axes of the slice: x: 2, y: 2, z: 4, core: 2. Of those that a mesh axis runs over, the one named last changes fastest.
Arguments:
- queries: bfloat16 [64, 64, 128], P(('req', 'exp'), 'head'), may hold values from -18 to 18
- keys: bfloat16 [64, 512, 4, 128], P(('req', 'exp'), None, 'head'), may hold values from -15 to 15
- values: bfloat16 [64, 512, 4, 128], P(('req', 'exp'), None, 'head'), may hold values from -12 to 12
- lengths: int32 [64], P(('req', 'exp')), may hold values from 1 to 512, as said below
- out_weight: bfloat16 [8192, 4096], P('head', 'exp'), may hold values from -0.0625 to 0.0625
- resid: bfloat16 [64, 4096], P('req', 'exp'), may hold values from -11 to 11
- norm_gain: float32 [4096], replicated, may hold values from 0.25 to 1.75
- expert_ids: int32 [64, 8], P('req'), may hold values from 0 to 15, all different within a row; in each aligned block of 16 rows (0 to 15, 16 to 31, ...) at most 8 rows name the same one
- route_weights: float32 [64, 8], P('req'), may hold values from 0.1 to 1
- w_gate: bfloat16 [16, 4096, 768], P(('req', 'exp'), None, 'head'), may hold values from -0.09375 to 0.09375
- w_up: bfloat16 [16, 4096, 768], P(('req', 'exp'), None, 'head'), may hold values from -0.09375 to 0.09375
- w_down: bfloat16 [16, 768, 4096], P(('req', 'exp'), 'head'), may hold values from -0.21875 to 0.21875
Outputs:
- layer_out: bfloat16 [64, 4096], P('req', 'exp')
Inputs may be any that keep to these rules, and one draw needn't show every extreme that they name: `expert_ids`: within each aligned block of 16 rows (the tokens of one index of req), a row names 8 different experts and no expert is named by more than 8 rows; some expert is named by exactly 8 rows. `lengths`: some question's cache is full.
All inputs are finite; a program needn't handle non-finite values.
Results may differ from a plain program's by a relative error of at most 0.0049.
Values may be sent and summed in bfloat16 or wider, within the bound.
No kernel may reach another device: no remote copies, remote signals or barrier semaphores. Data moves between devices by JAX's collectives and lax.ppermute only.
A program may use at most 64 MiB of HBM per device.

v0:
```python
import math
import jax
import jax.numpy as jnp
from jax import lax
from jax.sharding import PartitionSpec as P


def local(
    queries,
    keys,
    values,
    lengths,
    out_weight,
    resid,
    norm_gain,
    expert_ids,
    route_weights,
    w_gate,
    w_up,
    w_down,
):
    req_count = lax.axis_size("req")
    exp_count = lax.axis_size("exp")
    column = lax.axis_index("exp")
    rows_dev, heads_dev, head_size = queries.shape
    slots = keys.shape[1]
    kv_heads = keys.shape[2]
    group_rows, col_width = resid.shape
    full_width = norm_gain.shape[0]
    capacity = 2 * rows_dev
    expert_total = req_count * exp_count
    grouped_result = queries.reshape(rows_dev, kv_heads, heads_dev // kv_heads, head_size)
    logits = jnp.einsum(
        "rgjd,rcgd->rgjc", grouped_result, keys, preferred_element_type=jnp.float32
    ) * (1.0 / math.sqrt(head_size))
    visible = jnp.arange(slots, dtype=jnp.int32)[None, :] < lengths[:, None]
    logits = jnp.where(visible[:, None, None, :], logits, -1e30)
    peak = jnp.max(logits, axis=-1, keepdims=True)
    raised = jnp.exp(logits - peak)
    soft_weights = (raised / jnp.sum(raised, axis=-1, keepdims=True)).astype(jnp.bfloat16)
    attended = jnp.einsum(
        "rgjc,rcgd->rgjd", soft_weights, values, preferred_element_type=jnp.float32
    )
    attended = attended.reshape(rows_dev, heads_dev * head_size).astype(jnp.bfloat16)
    projected = jnp.dot(
        lax.all_gather(attended, "exp", axis=0, tiled=True),
        out_weight,
        preferred_element_type=jnp.float32,
    )
    projected = lax.psum(projected, "head")
    hidden = resid.astype(jnp.float32) + projected
    squares = lax.psum(jnp.sum(hidden * hidden, axis=1), "exp")
    inverse = lax.rsqrt(squares / full_width + 1e-06)
    gain_cols = lax.dynamic_slice_in_dim(norm_gain, column * col_width, col_width)
    normed_cols = (hidden * inverse[:, None] * gain_cols[None, :]).astype(jnp.bfloat16)
    matched = expert_ids[:, :, None] == jnp.arange(expert_total, dtype=jnp.int32)[None, None, :]
    chosen = jnp.any(matched, axis=1)
    weighting = jnp.sum(jnp.where(matched, route_weights[:, :, None], 0.0), axis=1)
    position = jnp.cumsum(chosen.astype(jnp.int32), axis=0) - 1
    selector = (
        position.T[:, None, :] == jnp.arange(capacity, dtype=jnp.int32)[None, :, None]
    ) & chosen.T[:, None, :]
    spread = jnp.where(selector, weighting.T[:, None, :], 0.0)
    outgoing = jnp.einsum(
        "ecg,gd->ecd",
        selector.astype(jnp.bfloat16),
        normed_cols,
        preferred_element_type=jnp.float32,
    ).astype(jnp.bfloat16)
    arrived = lax.all_to_all(outgoing, ("req", "exp"), split_axis=0, concat_axis=0, tiled=True)
    items = arrived.shape[1]
    rows = arrived.reshape(req_count, exp_count, items, col_width).transpose(0, 2, 1, 3)
    rows = rows.reshape(req_count, items, exp_count * col_width)
    gate_act = jnp.einsum("snd,df->snf", rows, w_gate[0], preferred_element_type=jnp.float32)
    up_act = jnp.einsum("snd,df->snf", rows, w_up[0], preferred_element_type=jnp.float32)
    activated = (jax.nn.silu(gate_act) * up_act).astype(jnp.bfloat16)
    expert_out = jnp.einsum("snf,fd->snd", activated, w_down[0], preferred_element_type=jnp.float32)
    expert_out = lax.psum(expert_out, "head")
    pieces = expert_out.reshape(req_count, items, exp_count, col_width).transpose(0, 2, 1, 3)
    pieces = pieces.reshape(req_count * exp_count, items, col_width)
    returned = lax.all_to_all(pieces, ("req", "exp"), split_axis=0, concat_axis=0, tiled=True)
    mixture = jnp.einsum("ecg,ecd->gd", spread, returned, precision=lax.Precision.HIGHEST)
    return (hidden + mixture).astype(jnp.bfloat16)


def solution(mesh):
    in_specs = (
        P(("req", "exp"), "head", None),
        P(("req", "exp"), None, "head", None),
        P(("req", "exp"), None, "head", None),
        P(("req", "exp")),
        P("head", "exp"),
        P("req", "exp"),
        P(),
        P("req", None),
        P("req", None),
        P(("req", "exp"), None, "head"),
        P(("req", "exp"), None, "head"),
        P(("req", "exp"), "head", None),
    )
    out_specs = P("req", "exp")
    return jax.shard_map(local, mesh=mesh, in_specs=in_specs, out_specs=out_specs, check_vma=False)
```

profile of v0, /device:TPU:0, one launch (start us, length us, event | category | flops | bytes accessed | tf_op | source)
XLA Modules:
  0.0 127.2 jit_solution(6337636310465268059)
XLA Ops:
  6.5 0.9 iota_compare_fusion.2
  7.4 1.7 %fusion.9 = f32[4,2,16,512]{3,2,1,0:T(8,128)S(1)} fusion(bf16[4,2,16,128]{3,2,1,0:T(8,128)(2,1)} %bitcast.52, bf16[4,512,2,128]{3,2,1,0:T(2,128)(2,1)} %param.13, pred[4,512]{1,0:T(4,128)(4,1)S(1)} %iota_compare_fusion.2), kind=kOutput, calls=%fused_computation.11 | convolution fusion | flops 16908288 | bytes 1345536 | tf_op jit(solution)/shard_map/rgjd,rcgd->rgjc/dot_general | solution.py:33
  9.1 0.2 fusion.44
  9.3 1.5 %convolution_convert_fusion.1 = bf16[4,2,16,128]{3,2,1,0:T(8,128)(2,1)S(1)} fusion(bf16[4,512,2,128]{3,2,1,0:T(2,128)(2,1)} %param.14, f32[4,2,16]{2,1,0:T(2,128)S(1)} %fusion.44, f32[4,2,16,512]{3,2,1,0:T(8,128)S(1)} %fusion.9), kind=kOutput, calls=%fused_computation.16 | convolution fusion | flops 16990848 | bytes 1344000 | tf_op jit(solution)/shard_map/rgjc,rcgd->rgjd/dot_general | solution.py:41
  10.9 9.9 %all-gather = bf16[4,4,4096]{2,1,0:T(4,128)(2,1)S(1)} all-gather(bf16[1,4,4096]{2,1,0:T(4,128)(2,1)S(1)} %reshape.45), channel_id=1, replica_groups=mesh['req'=4,'head'=2,'exp'=4] {'exp'}, dimensions={0}, use_global_device_ids=true | all-gather | bytes 163840 | tf_op jit(solution)/shard_map/all_gather | solution.py:46
  20.9 5.2 %fusion.45 = f32[16,1024]{1,0:T(8,128)} fusion(bf16[16,4096]{1,0:T(8,128)(2,1)S(1)} %reshape.46, bf16[4096,1024]{1,0:T(8,128)(2,1)} %param.16), kind=kOutput, calls=%fused_computation.52 | convolution fusion | flops 134217728 | bytes 8585216 | tf_op jit(solution)/shard_map/dot_general | solution.py:45
  26.2 0.1 copy.19
  26.4 0.1 copy.20
  26.5 0.1 copy.22
  26.6 17.7 %all-reduce.3.cloned.1.call-done = f32[16,1024]{1,0:T(8,128)} async-done(((f32[16,1024]{1,0:T(8,128)}), f32[16,1024]{1,0:T(8,128)}) %all-reduce.3.cloned.1.call-update) | async-done | bytes 65552 | tf_op jit(solution)/shard_map/psum | solution.py:50
  44.3 1.0 multiply_reduce_fusion
  45.3 0.7 dynamic_slice.3
  46.0 10.1 %psum.22 = f32[16]{0:T(128)S(1)} all-reduce(f32[16]{0:T(128)S(1)} %multiply_reduce_fusion), channel_id=1, replica_groups=mesh['req'=4,'head'=2,'exp'=4] {'exp'}, use_global_device_ids=true, to_apply=%region_7.8 | all-reduce | flops 16 | bytes 128 | tf_op jit(solution)/shard_map/psum | solution.py:52
  56.1 1.1 convolution_convert_fusion
  57.2 13.0 %all_to_all.10 = bf16[16,8,1024]{2,1,0:T(8,128)(2,1)S(1)} all-to-all(bf16[16,8,1024]{2,1,0:T(8,128)(2,1)S(1)} %convolution_convert_fusion), channel_id=1, replica_groups=mesh['req'=4,'head'=2,'exp'=4] {'req','exp'}, dimensions={0} | all-to-all | bytes 524288 | tf_op jit(solution)/shard_map/all_to_all | solution.py:70
  70.2 2.4 %fusion.5 = f32[4,8,384]{2,1,0:T(8,128)S(1)} fusion(bf16[4,8,4096]{2,1,0:T(8,128)(2,1)S(1)} %bitcast.48, bf16[1,4096,384]{2,1,0:T(8,128)(2,1)} %param.21), kind=kOutput, calls=%fused_computation.5 | convolution fusion | flops 100663296 | bytes 3457024 | tf_op jit(solution)/shard_map/snd,df->snf/dot_general | solution.py:74
  72.7 4.1 %fusion.1 = f32[4,8,4096]{2,1,0:T(8,128)} fusion(bf16[1,384,4096]{2,1,0:T(8,128)(2,1)S(1)} %copy-done, bf16[4,8,4096]{2,1,0:T(8,128)(2,1)S(1)} %bitcast.49, bf16[1,4096,384]{2,1,0:T(8,128)(2,1)} %param.22, f32[4,8,384]{2,1,0:T(8,128)S(1)} %fusion.5), kind=kOutput, calls=%fused_computation.1 | convolution fusion | flops 201400320 | bytes 7127040 | tf_op jit(solution)/shard_map/snf,fd->snd/dot_general | solution.py:77
  76.8 16.7 %all-reduce.5.cloned.1.call-done = f32[4,8,4096]{2,1,0:T(8,128)} async-done(((f32[4,8,4096]{2,1,0:T(8,128)}), f32[4,8,4096]{2,1,0:T(8,128)}) %all-reduce.5.cloned.1.call-update) | async-done | bytes 524304 | tf_op jit(solution)/shard_map/psum | solution.py:78
  93.4 1.1 fusion.43
  94.6 0.8 pad_maximum_fusion
  95.4 6.9 %all-to-all-start.1 = ((f32[16,8,1024]{2,1,0:T(8,128)}), f32[16,8,1024]{2,1,0:T(8,128)}, u32[]{:S(2)}, u32[]{:S(2)}) async-start(f32[16,8,1024]{2,1,0:T(8,128)} %bitcast.50), calls=%async_computation.1 | async-start | bytes 1048576 | tf_op jit(solution)/shard_map/all_to_all | solution.py:81
  102.3 0.1 copy.21
  102.4 15.4 %all-to-all-done.1 = f32[16,8,1024]{2,1,0:T(8,128)} async-done(((f32[16,8,1024]{2,1,0:T(8,128)}), f32[16,8,1024]{2,1,0:T(8,128)}, u32[]{:S(2)}, u32[]{:S(2)}) %all-to-all-start.1) | async-done | bytes 524320 | tf_op jit(solution)/shard_map/all_to_all | solution.py:81
  117.9 2.5 %fusion.14 = bf16[16,1024]{1,0:T(8,128)(2,1)} fusion(f32[16,8,1024]{2,1,0:T(8,128)} %all-to-all-done.1, f32[16,16]{0,1:T(8,128)S(1)} %copy.21, f32[16,1024]{1,0:T(8,128)S(1)} %copy-done.1, bf16[16,1024]{1,0:T(8,128)(2,1)S(1)} %copy-done.2, s32[16,16]{0,1:T(8,128)S(1)} %add_bitcast_fusion, pred[16,16]{0,1:T(8,128)(4,1)S(1)} %copy.20), kind=kOutput, calls=%fused_computation.15 | convolution fusion | flops 25237504 | bytes 657664 | tf_op jit(solution)/shard_map/ecg,ecd->gd/dot_general | solution.py:82
  (23 shorter events, 0.3 us)
Async XLA Ops:
  6.5 66.1 %copy-start = (bf16[1,384,4096]{2,1,0:T(8,128)(2,1)S(1)}, bf16[1,384,4096]{2,1,0:T(8,128)(2,1)}, u32[]{:S(2)}) copy-start(bf16[1,384,4096]{2,1,0:T(8,128)(2,1)} %param.23) | copy-start | bytes 9437188
  6.5 37.8 %all-reduce.3.cloned.1.call-start = ((), (), s32[]{:S(2)}) async-start(), calls=%async_computation.2 | async-start | bytes 131072 | tf_op jit(solution)/shard_map/psum | solution.py:50
  20.9 5.3 %copy-start.3 = (s32[16,8]{0,1:T(8,128)S(1)}, s32[16,8]{0,1:T(8,128)}, u32[]{:S(2)}) copy-start(s32[16,8]{0,1:T(8,128)} %param.19) | copy-start | bytes 1540
  20.9 23.4 %copy-start.2 = (bf16[16,1024]{1,0:T(8,128)(2,1)S(1)}, bf16[16,1024]{1,0:T(8,128)(2,1)}, u32[]{:S(2)}) copy-start(bf16[16,1024]{1,0:T(8,128)(2,1)} %param.17) | copy-start | bytes 98308
  26.1 67.3 %all-reduce.5.cloned.1.call-start = ((), (), s32[]{:S(2)}) async-start(), calls=%async_computation.3 | async-start | bytes 1048576 | tf_op jit(solution)/shard_map/psum | solution.py:78
  76.8 25.6 %copy-start.4 = (f32[16,8]{0,1:T(8,128)S(1)}, f32[16,8]{0,1:T(8,128)}, u32[]{:S(2)}) copy-start(f32[16,8]{0,1:T(8,128)} %param.20) | copy-start | bytes 1540
  76.8 41.1 %copy-start.1 = (f32[16,1024]{1,0:T(8,128)S(1)}, f32[16,1024]{1,0:T(8,128)}, u32[]{:S(2)}) copy-start(f32[16,1024]{1,0:T(8,128)} %all-reduce.3.cloned.1.call-done) | copy-start | bytes 196612
  95.4 22.4 %all-to-all-start.1 = ((f32[16,8,1024]{2,1,0:T(8,128)}), f32[16,8,1024]{2,1,0:T(8,128)}, u32[]{:S(2)}, u32[]{:S(2)}) async-start(f32[16,8,1024]{2,1,0:T(8,128)} %bitcast.50), calls=%async_computation.1 | async-start | bytes 1048576 | tf_op jit(solution)/shard_map/all_to_all | solution.py:81
Sparse Core Ops, SparseCore 0:
  26.3 17.9 all-reduce.2
  76.9 16.4 all-reduce.4
where the time goes:
time: 128 us; the launch traced here: 127 us
  waiting for transfers between devices  49.9 us (39%)
  blocking collectives  33.1 us (26%)
  matrix products  18.6 us (15%)
  between operations  13.5 us (11%)
  starting transfers between devices  6.92 us (5%)
  other arithmetic  3 us (2%)
  local copies, waits for them, and re-layouts  2.23 us (2%)
    psum x1, waiting for transfers between devices, local(): projected = lax.psum(projected, 'head')  17.7 us
    psum x1, waiting for transfers between devices, local(): expert_out = lax.psum(expert_out, 'head')  16.7 us
    all_to_all x1, waiting for transfers between devices, local(): lax.all_to_all(pieces, ('req', 'exp'), split_axis=0, concat_axis=0, tiled...  15.4 us
    all_to_all x1, blocking collectives, local(): lax.all_to_all(outgoing, ('req', 'exp'), split_axis=0, concat_axis=0, til...  13 us
    psum x1, blocking collectives, local(): squares = lax.psum(jnp.sum(hidden * hidden, axis=1), 'exp')  10.1 us
    all_gather x1, blocking collectives, local(): lax.all_gather(attended, 'exp', axis=0, tiled=True)  9.94 us
    all_to_all x1, starting transfers between devices, local(): lax.all_to_all(pieces, ('req', 'exp'), split_axis=0, concat_axis=0, tiled...  6.88 us
    dot_general x1, matrix products, local(): jnp.dot(lax.all_gather(attended, 'exp', axis=0, tiled=True), out_weight,...  5.21 us
  transfers between devices with their start and end apart: 3, of which 3 were waited for; matrix products, arithmetic and copies ran while one was open for 0% of the time, Pallas kernels for 0%

commit v1 on v0

--- a/solution.py
+++ b/solution.py
@@ -1,8 +1,17 @@
+import functools
 import math
 import jax
 import jax.numpy as jnp
 from jax import lax
 from jax.sharding import PartitionSpec as P
+
+
+def switch_inputs_on_mesh(sample, shard_axis):
+    after = lax.all_gather(sample, shard_axis)
+    return jnp.sum(after, axis=0)
+
+
+group_quotas = functools.partial(switch_inputs_on_mesh, shard_axis="head")
 
 
 def local(
@@ -47,7 +56,7 @@
         out_weight,
         preferred_element_type=jnp.float32,
     )
-    projected = lax.psum(projected, "head")
+    projected = group_quotas(projected)
     hidden = resid.astype(jnp.float32) + projected
     squares = lax.psum(jnp.sum(hidden * hidden, axis=1), "exp")
     inverse = lax.rsqrt(squares / full_width + 1e-06)

time: 128 us -> 110 us (0.86)
  waiting for transfers between devices: 49.9 us -> 32.1 us
  blocking collectives: 33.1 us -> 35 us
  matrix products: 18.6 us -> 17.2 us
    psum x1 -> x0, waiting for transfers between devices: 17.7 us -> none  [local(): projected = lax.psum(projected, 'head')]
    all_gather x0 -> x1, blocking collectives: none -> 1.9 us  [switch_inputs_on_mesh(): after = lax.all_gather(sample, shard_axis)]
  transfers between devices with their start and end apart: 3 -> 2, of which waited for: 3 -> 2; matrix products, arithmetic and copies ran while one was open for 0% -> 0% of each run, Pallas kernels for 0% -> 0%
where the time goes in v1:
time: 110 us
  blocking collectives  35 us (32%)
  waiting for transfers between devices  32.1 us (29%)
  matrix products  17.2 us (16%)
  between operations  13.5 us (12%)
  starting transfers between devices  6.88 us (6%)
  local copies, waits for them, and re-layouts  2.83 us (3%)
  other arithmetic  2.17 us (2%)
    psum x1, waiting for transfers between devices, local(): expert_out = lax.psum(expert_out, 'head')  16.6 us
    all_to_all x1, waiting for transfers between devices, local(): lax.all_to_all(pieces, ('req', 'exp'), split_axis=0, concat_axis=0, tiled...  15.4 us
    all_to_all x1, blocking collectives, local(): lax.all_to_all(outgoing, ('req', 'exp'), split_axis=0, concat_axis=0, til...  14.2 us
    all_gather x1, blocking collectives, local(): lax.all_gather(attended, 'exp', axis=0, tiled=True)  9.94 us
    psum x1, blocking collectives, local(): squares = lax.psum(jnp.sum(hidden * hidden, axis=1), 'exp')  8.95 us
    all_to_all x1, starting transfers between devices, local(): lax.all_to_all(pieces, ('req', 'exp'), split_axis=0, concat_axis=0, tiled...  6.88 us
    dot_general x1, matrix products, local(): jnp.dot(lax.all_gather(attended, 'exp', axis=0, tiled=True), out_weight,...  4.58 us
    dot_general x1, matrix products, local(): jnp.einsum('snf,fd->snd', activated, w_down[0], preferred_element_type=jn...  4.09 us
  transfers between devices with their start and end apart: 2, of which 2 were waited for; matrix products, arithmetic and copies ran while one was open for 0% of the time, Pallas kernels for 0%

profile of v1, /device:TPU:0, one launch (start us, length us, event | category | flops | bytes accessed | tf_op | source)
XLA Modules:
  0.0 109.6 jit_solution(2851812561246986492)
XLA Ops:
  6.5 0.9 iota_compare_fusion.2
  7.4 1.7 %fusion.9 = f32[4,2,16,512]{3,2,1,0:T(8,128)S(1)} fusion(bf16[4,2,16,128]{3,2,1,0:T(8,128)(2,1)} %bitcast.54, bf16[4,512,2,128]{3,2,1,0:T(2,128)(2,1)} %param.13, pred[4,512]{1,0:T(4,128)(4,1)S(1)} %iota_compare_fusion.2), kind=kOutput, calls=%fused_computation.11 | convolution fusion | flops 16908288 | bytes 1345536 | tf_op jit(solution)/shard_map/rgjd,rcgd->rgjc/dot_general | solution.py:42
  9.1 0.2 fusion.44
  9.3 1.5 %convolution_convert_fusion.1 = bf16[4,2,16,128]{3,2,1,0:T(8,128)(2,1)S(1)} fusion(bf16[4,512,2,128]{3,2,1,0:T(2,128)(2,1)} %param.14, f32[4,2,16]{2,1,0:T(2,128)S(1)} %fusion.44, f32[4,2,16,512]{3,2,1,0:T(8,128)S(1)} %fusion.9), kind=kOutput, calls=%fused_computation.16 | convolution fusion | flops 16990848 | bytes 1344000 | tf_op jit(solution)/shard_map/rgjc,rcgd->rgjd/dot_general | solution.py:50
  10.9 9.9 %all-gather.1 = bf16[4,4,4096]{2,1,0:T(4,128)(2,1)S(1)} all-gather(bf16[1,4,4096]{2,1,0:T(4,128)(2,1)S(1)} %reshape.46), channel_id=1, replica_groups=mesh['req'=4,'head'=2,'exp'=4] {'exp'}, dimensions={0}, use_global_device_ids=true | all-gather | bytes 163840 | tf_op jit(solution)/shard_map/all_gather | solution.py:55
  20.9 4.6 %fusion.45 = f32[16,1024]{1,0:T(8,128)S(1)} fusion(bf16[16,4096]{1,0:T(8,128)(2,1)S(1)} %reshape.47, bf16[4096,1024]{1,0:T(8,128)(2,1)} %param.16), kind=kOutput, calls=%fused_computation.52 | convolution fusion | flops 134217728 | bytes 8585216 | tf_op jit(solution)/shard_map/dot_general | solution.py:54
  25.5 1.9 %all-gather = f32[32,1024]{1,0:T(8,128)S(1)} all-gather(f32[16,1024]{1,0:T(8,128)S(1)} %fusion.45), channel_id=2, replica_groups=mesh['req'=4,'head'=2,'exp'=4] {'head'}, dimensions={0}, use_global_device_ids=true | all-gather | bytes 196608 | tf_op jit(solution)/shard_map/all_gather | solution.py:10
  27.4 0.1 multiply_reduce_fusion
  27.5 9.0 %psum.14 = f32[16]{0:T(128)S(1)} all-reduce(f32[16]{0:T(128)S(1)} %multiply_reduce_fusion), channel_id=1, replica_groups=mesh['req'=4,'head'=2,'exp'=4] {'exp'}, use_global_device_ids=true, to_apply=%region_7.8 | all-reduce | flops 16 | bytes 128 | tf_op jit(solution)/shard_map/psum | solution.py:61
  36.5 0.1 copy.19
  36.7 0.1 copy.20
  36.8 0.6 copy-done.4
  37.4 0.1 copy.22
  37.5 0.7 dynamic_slice.3
  38.2 0.3 convolution_convert_fusion
  38.4 14.2 %all_to_all.10 = bf16[16,8,1024]{2,1,0:T(8,128)(2,1)S(1)} all-to-all(bf16[16,8,1024]{2,1,0:T(8,128)(2,1)S(1)} %convolution_convert_fusion), channel_id=1, replica_groups=mesh['req'=4,'head'=2,'exp'=4] {'req','exp'}, dimensions={0} | all-to-all | bytes 524288 | tf_op jit(solution)/shard_map/all_to_all | solution.py:79
  52.6 2.4 %fusion.5 = f32[4,8,384]{2,1,0:T(8,128)S(1)} fusion(bf16[4,8,4096]{2,1,0:T(8,128)(2,1)S(1)} %bitcast.49, bf16[1,4096,384]{2,1,0:T(8,128)(2,1)} %param.21), kind=kOutput, calls=%fused_computation.5 | convolution fusion | flops 100663296 | bytes 3457024 | tf_op jit(solution)/shard_map/snd,df->snf/dot_general | solution.py:83
  55.1 4.1 %fusion.1 = f32[4,8,4096]{2,1,0:T(8,128)} fusion(bf16[1,384,4096]{2,1,0:T(8,128)(2,1)S(1)} %copy-done, bf16[4,8,4096]{2,1,0:T(8,128)(2,1)S(1)} %bitcast.50, bf16[1,4096,384]{2,1,0:T(8,128)(2,1)} %param.22, f32[4,8,384]{2,1,0:T(8,128)S(1)} %fusion.5), kind=kOutput, calls=%fused_computation.1 | convolution fusion | flops 201400320 | bytes 7127040 | tf_op jit(solution)/shard_map/snf,fd->snd/dot_general | solution.py:86
  59.2 16.6 %all-reduce.2.cloned.1.call-done = f32[4,8,4096]{2,1,0:T(8,128)} async-done(((f32[4,8,4096]{2,1,0:T(8,128)}), f32[4,8,4096]{2,1,0:T(8,128)}) %all-reduce.2.cloned.1.call-update) | async-done | bytes 524304 | tf_op jit(solution)/shard_map/psum | solution.py:87
  75.8 1.1 %fusion.43 = (f32[4,8,1024]{2,1,0:T(8,128)S(1)}, f32[4,8,1024]{2,1,0:T(8,128)S(1)}, f32[4,8,1024]{2,1,0:T(8,128)S(1)}, f32[4,8,1024]{2,1,0:T(8,128)S(1)}) fusion(f32[4,8,4096]{2,1,0:T(8,128)} %all-reduce.2.cloned.1.call-done), kind=kLoop, calls=%fused_computation.50 | loop fusion | bytes 1048576 | tf_op jit(solution)/shard_map/slice
  77.0 0.8 pad_maximum_fusion
  77.8 6.9 %all-to-all-start.1 = ((f32[16,8,1024]{2,1,0:T(8,128)}), f32[16,8,1024]{2,1,0:T(8,128)}, u32[]{:S(2)}, u32[]{:S(2)}) async-start(f32[16,8,1024]{2,1,0:T(8,128)} %bitcast.51), calls=%async_computation.1 | async-start | bytes 1048576 | tf_op jit(solution)/shard_map/all_to_all | solution.py:90
  84.8 15.4 %all-to-all-done.1 = f32[16,8,1024]{2,1,0:T(8,128)} async-done(((f32[16,8,1024]{2,1,0:T(8,128)}), f32[16,8,1024]{2,1,0:T(8,128)}, u32[]{:S(2)}, u32[]{:S(2)}) %all-to-all-start.1) | async-done | bytes 524320 | tf_op jit(solution)/shard_map/all_to_all | solution.py:90
  100.2 2.5 %fusion.14 = bf16[16,1024]{1,0:T(8,128)(2,1)} fusion(f32[16,8,1024]{2,1,0:T(8,128)} %all-to-all-done.1, f32[16,16]{0,1:T(8,128)S(1)} %copy.21, f32[16,1024]{1,0:T(8,128)S(1)} %reduce_sum.37, bf16[16,1024]{1,0:T(8,128)(2,1)S(1)} %copy-done.1, s32[16,16]{0,1:T(8,128)S(1)} %copy-done.3, pred[16,16]{0,1:T(8,128)(4,1)S(1)} %copy-done.5), kind=kOutput, calls=%fused_computation.15 | convolution fusion | flops 25237504 | bytes 657664 | tf_op jit(solution)/shard_map/ecg,ecd->gd/dot_general | solution.py:91
  (30 shorter events, 0.3 us)
Async XLA Ops:
  6.5 48.5 %copy-start = (bf16[1,384,4096]{2,1,0:T(8,128)(2,1)S(1)}, bf16[1,384,4096]{2,1,0:T(8,128)(2,1)}, u32[]{:S(2)}) copy-start(bf16[1,384,4096]{2,1,0:T(8,128)(2,1)} %param.23) | copy-start | bytes 9437188
  6.5 69.3 %all-reduce.2.cloned.1.call-start = ((), (), s32[]{:S(2)}) async-start(), calls=%async_computation.2 | async-start | bytes 1048576 | tf_op jit(solution)/shard_map/psum | solution.py:87
  20.9 6.5 %copy-start.1 = (bf16[16,1024]{1,0:T(8,128)(2,1)S(1)}, bf16[16,1024]{1,0:T(8,128)(2,1)}, u32[]{:S(2)}) copy-start(bf16[16,1024]{1,0:T(8,128)(2,1)} %param.17) | copy-start | bytes 98308
  20.9 15.6 %copy-start.6 = (s32[16,8]{0,1:T(8,128)S(1)}, s32[16,8]{0,1:T(8,128)}, u32[]{:S(2)}) copy-start(s32[16,8]{0,1:T(8,128)} %param.19) | copy-start | bytes 1540
  36.7 1.5 %copy-start.2 = (s32[16,16]{0,1:T(8,128)}, s32[16,16]{0,1:T(8,128)S(1)}, u32[]{:S(2)}) copy-start(s32[16,16]{0,1:T(8,128)S(1)} %add_bitcast_fusion) | copy-start | bytes 3076
  36.8 0.6 copy-start.4
  59.2 25.5 %copy-start.7 = (s32[16,8]{0,1:T(8,128)S(1)}, s32[16,8]{0,1:T(8,128)}, u32[]{:S(2)}) copy-start(s32[16,8]{0,1:T(8,128)} %param.19) | copy-start | bytes 1540
  59.2 25.6 %copy-start.8 = (f32[16,8]{0,1:T(8,128)S(1)}, f32[16,8]{0,1:T(8,128)}, u32[]{:S(2)}) copy-start(f32[16,8]{0,1:T(8,128)} %param.20) | copy-start | bytes 1540
  59.2 41.1 %copy-start.3 = (s32[16,16]{0,1:T(8,128)S(1)}, s32[16,16]{0,1:T(8,128)}, u32[]{:S(2)}) copy-start(s32[16,16]{0,1:T(8,128)} %copy-done.2) | copy-start | bytes 3076
  59.2 41.1 %copy-start.5 = (pred[16,16]{0,1:T(8,128)(4,1)S(1)}, pred[16,16]{0,1:T(8,128)(4,1)}, u32[]{:S(2)}) copy-start(pred[16,16]{0,1:T(8,128)(4,1)} %copy-done.4) | copy-start | bytes 772
  77.8 22.4 %all-to-all-start.1 = ((f32[16,8,1024]{2,1,0:T(8,128)}), f32[16,8,1024]{2,1,0:T(8,128)}, u32[]{:S(2)}, u32[]{:S(2)}) async-start(f32[16,8,1024]{2,1,0:T(8,128)} %bitcast.51), calls=%async_computation.1 | async-start | bytes 1048576 | tf_op jit(solution)/shard_map/all_to_all | solution.py:90
Sparse Core Ops, SparseCore 0:
  59.3 16.4 all-reduce.1
